TPU v7x, 512 devices: a whole 4x8x8 slice. The times are simulated.
512 devices in a mesh: dp: 64 (over z, x, core), expert: 8 (over y).
Axes of the slice: x: 4, y: 8, z: 8, core: 2. Of those that a mesh axis runs over, the one named last changes fastest.
Arguments:
- tokens: bfloat16 [512, 4096], P('expert', 'dp'), may hold values from -6 to 6
- cotangent: bfloat16 [512, 4096], P('expert', 'dp'), may hold values from -6 to 6
- gate_logit: float32 [512], P('expert'), may hold values from -8 to 8
- routes: int32 [512, 2], P('expert'), may hold values from 0 to 7, all different within a row; in each aligned block of 64 rows (0 to 63, 64 to 127, ...) at most 32 rows name the same one
- w_up: bfloat16 [8, 14336, 4096], P('expert', 'dp'), may hold values from -0.09375 to 0.09375
- w_down: bfloat16 [8, 14336, 4096], P('expert', 'dp'), may hold values from -0.046875 to 0.046875
- basis: bfloat16 [4096, 256], P('dp'), may hold values from -0.09375 to 0.09375
- sketch: float32 [8, 256, 256], P('expert'), may hold values from -1 to 10, as said below
Outputs:
- token_grad: bfloat16 [512, 4096], P('expert', 'dp')
- sketch_next: float32 [8, 256, 256], P('expert')
- precond: float32 [8, 14336, 256], P('expert', 'dp')
Inputs may be any that keep to these rules, and one draw needn't show every extreme that they name: `routes`: each row names 2 different experts. Among the 64 tokens of one index of expert at most 32 name the same expert, and in some index that many do. `sketch`: each matrix is symmetric, and in every row its diagonal entry exceeds the sum of the magnitudes off the diagonal.
All inputs are finite; a program needn't handle non-finite values.
Results may differ from a plain program's by a relative error of at most 0.0064.
Values may be sent and summed in bfloat16 or wider, within the bound.
A program may use at most 128 MiB of HBM per device.

v0:
```python
import jax
import jax.numpy as jnp
from jax import lax
from jax.sharding import PartitionSpec as P

decay_rate = 0.9
damping = 1.0
highest = lax.Precision.HIGHEST


def per_device(tokens, cotangent, gate_logit, routes, w_up, w_down, basis, sketch):
    experts = lax.axis_size("expert")
    tok_rows = tokens.shape[0]
    width_local = tokens.shape[1]
    capacity = min(tok_rows, tok_rows * 4 // experts)
    slot_count = experts * capacity
    gate_first = jax.nn.sigmoid(gate_logit)
    gates = jnp.stack([gate_first, 1.0 - gate_first], axis=1)
    expert_ids = jnp.arange(experts, dtype=jnp.int32)
    chosen = routes[:, :, None] == expert_ids[None, None, :]
    hit_count = jnp.sum(chosen.astype(jnp.int32), axis=1)
    gate_by_expert = jnp.sum(chosen.astype(jnp.float32) * gates[:, :, None], axis=1)
    before = jnp.cumsum(hit_count, axis=0) - hit_count
    slot_of = expert_ids[None, :] * capacity + before
    slot_ids = jnp.arange(slot_count, dtype=jnp.int32)
    slot_match = (
        (slot_of[None, :, :] == slot_ids[:, None, None]) & (hit_count[None, :, :] > 0)
    ).astype(jnp.float32)
    table = jnp.sum(slot_match, axis=2)
    gate_slot = jnp.sum(slot_match * gate_by_expert[None, :, :], axis=(1, 2))
    table_b = table.astype(jnp.bfloat16)
    x_send = jnp.dot(table_b, tokens, preferred_element_type=jnp.float32).astype(jnp.bfloat16)
    cot_rows = jnp.dot(table_b, cotangent, preferred_element_type=jnp.float32)
    dy_send = (gate_slot[:, None] * cot_rows).astype(jnp.bfloat16)
    x_send = x_send.reshape(experts, capacity, width_local)
    dy_send = dy_send.reshape(experts, capacity, width_local)
    x_recv, dy_recv = (
        lax.all_to_all(x_send, "expert", split_axis=0, concat_axis=0, tiled=True),
        lax.all_to_all(dy_send, "expert", split_axis=0, concat_axis=0, tiled=True),
    )
    x_full, dy_full = (
        lax.all_gather(x_recv, "dp", axis=2, tiled=True),
        lax.all_gather(dy_recv, "dp", axis=2, tiled=True),
    )
    row_block = x_full.reshape(slot_count, -1)
    dy_block = dy_full.reshape(slot_count, -1)
    up_local = w_up[0]
    down_local = w_down[0]
    hidden = lax.dot_general(
        row_block, up_local, (((1,), (1,)), ((), ())), preferred_element_type=jnp.float32
    )
    back_grad = lax.dot_general(
        dy_block, down_local, (((1,), (1,)), ((), ())), preferred_element_type=jnp.float32
    )
    sigma_val = jax.nn.sigmoid(hidden)
    hidden_grad = (back_grad * sigma_val * (1.0 + hidden * (1.0 - sigma_val))).astype(jnp.bfloat16)
    partial_value = jnp.dot(hidden_grad, up_local, preferred_element_type=jnp.float32)
    summed = lax.psum_scatter(partial_value, "dp", scatter_dimension=1, tiled=True).astype(
        jnp.bfloat16
    )
    returned = lax.all_to_all(
        summed.reshape(experts, capacity, width_local),
        "expert",
        split_axis=0,
        concat_axis=0,
        tiled=True,
    )
    token_grad = lax.dot_general(
        table_b,
        returned.reshape(slot_count, width_local),
        (((0,), (0,)), ((), ())),
        preferred_element_type=jnp.float32,
    ).astype(jnp.bfloat16)
    basis_full = lax.all_gather(basis, "dp", axis=0, tiled=True)
    projected = jnp.dot(row_block, basis_full, preferred_element_type=jnp.float32).astype(
        jnp.bfloat16
    )
    coefficients = lax.dot_general(
        projected, hidden_grad, (((0,), (0,)), ((), ())), preferred_element_type=jnp.float32
    )
    gram_part = jnp.dot(coefficients, coefficients.T, precision=highest)
    total_hidden = w_up.shape[1] * lax.axis_size("dp")
    gram_total = lax.psum(gram_part, "dp") / total_hidden
    merged = decay_rate * sketch[0] + gram_total
    factor = jnp.linalg.cholesky(merged + damping * jnp.eye(merged.shape[0], dtype=jnp.float32))
    solved = damping * jax.scipy.linalg.cho_solve((factor, True), coefficients)
    return (token_grad, merged[None], solved.T[None])


def solution(mesh):
    in_specs = (
        P("expert", "dp"),
        P("expert", "dp"),
        P("expert"),
        P("expert", None),
        P("expert", "dp", None),
        P("expert", "dp", None),
        P("dp", None),
        P("expert", None, None),
    )
    out_specs = (P("expert", "dp"), P("expert", None, None), P("expert", "dp", None))
    return jax.shard_map(
        per_device, mesh=mesh, in_specs=in_specs, out_specs=out_specs, check_vma=False
    )
```

profile of v0, /device:TPU:2, one launch (start us, length us, event | category | flops | bytes accessed | tf_op | source)
XLA Modules:
  0.0 657.5 jit_solution(2081533431602891325)
XLA Ops:
  7.2 0.8 convert_reduce_fusion.1
  10.1 0.9 fusion.16
  11.3 14.9 %all_to_all.15 = bf16[8,2,1024]{2,1,0:T(2,128)(2,1)S(1)} all-to-all(bf16[8,2,1024]{2,1,0:T(2,128)(2,1)S(1)} %reshape.113), channel_id=1, replica_groups=mesh['dp'=64,'expert'=8] {'expert'}, dimensions={0} | all-to-all | bytes 65536 | tf_op jit(solution)/shard_map/all_to_all | solution.py:39
  26.3 0.8 copy.44
  27.2 0.9 convolution_convert_fusion.1
  28.3 10.4 %all_to_all.16 = bf16[8,2,1024]{2,1,0:T(2,128)(2,1)S(1)} all-to-all(bf16[8,2,1024]{2,1,0:T(2,128)(2,1)S(1)} %reshape.115), channel_id=1, replica_groups=mesh['dp'=64,'expert'=8] {'expert'}, dimensions={0} | all-to-all | bytes 65536 | tf_op jit(solution)/shard_map/all_to_all | solution.py:38
  38.9 0.8 copy.47
  40.5 74.2 %all-gather.4.cloned.1.call-done = bf16[8,32,4096]{1,0,2:T(8,128)(2,1)} async-done(((bf16[8,32,64]{1,0,2:T(8,128)(2,1)}), bf16[8,32,4096]{1,0,2:T(8,128)(2,1)}) %all-gather.4.cloned.1.call-update) | async-done | bytes 2097168 | tf_op jit(solution)/shard_map/all_gather | solution.py:43
  114.7 9.3 %copy.45 = bf16[8,32,4096]{2,1,0:T(8,128)(2,1)} copy(bf16[8,32,4096]{1,0,2:T(8,128)(2,1)} %all-gather.4.cloned.1.call-done) | data formatting | bytes 4194304 | tf_op jit(solution)/shard_map/all_gather | solution.py:43
  124.0 80.1 %all-gather.6.cloned.1.call-done = bf16[8,32,4096]{1,0,2:T(8,128)(2,1)} async-done(((bf16[8,32,64]{1,0,2:T(8,128)(2,1)}), bf16[8,32,4096]{1,0,2:T(8,128)(2,1)}) %all-gather.6.cloned.1.call-update) | async-done | bytes 2097168 | tf_op jit(solution)/shard_map/all_gather | solution.py:42
  204.1 9.4 %copy.48 = bf16[8,32,4096]{2,1,0:T(8,128)(2,1)} copy(bf16[8,32,4096]{1,0,2:T(8,128)(2,1)} %all-gather.6.cloned.1.call-done) | data formatting | bytes 4194304 | tf_op jit(solution)/shard_map/all_gather | solution.py:42
  213.5 2.5 fusion.2
  216.3 0.8 fusion.12
  217.1 70.8 %all-gather.8.cloned.1.call-done = bf16[4096,256]{1,0:T(8,128)(2,1)} async-done(((bf16[64,256]{1,0:T(8,128)(2,1)}), bf16[4096,256]{1,0:T(8,128)(2,1)}) %all-gather.8.cloned.1.call-update) | async-done | bytes 2097168 | tf_op jit(solution)/shard_map/all_gather | solution.py:74
  287.8 3.1 fusion.15
  291.0 1.3 fusion.34
  292.6 2.9 fusion
  295.5 0.9 copy-done.2
  296.6 181.5 %all-reduce.3.cloned.1.call-done = f32[256,256]{0,1:T(8,128)} async-done(((f32[256,256]{0,1:T(8,128)}), f32[256,256]{0,1:T(8,128)}) %all-reduce.3.cloned.1.call-update) | async-done | bytes 262160 | tf_op jit(solution)/shard_map/psum | solution.py:83
  478.1 1.0 convert_add_fusion
  479.3 11.7 %cholesky.50 = f32[128,128]{1,0:T(8,128)S(1)} custom-call(f32[128,128]{1,0:T(8,128)S(1)} %cholesky.118), custom_call_target="Cholesky" | custom-call | tf_op jit(solution)/shard_map/jit(cholesky)/cholesky | solution.py:85
  491.0 9.8 %custom-call.18 = f32[1,128,128]{1,2,0:T(8,128)S(1)} custom-call(f32[1,128,128]{2,1,0:T(8,128)S(1)} %get-tuple-element.42), custom_call_target="InvertDiagBlocksLowerTriangular" | custom-call | tf_op jit(solution)/shard_map/jit(cholesky)/cholesky | solution.py:85
  501.3 11.7 %cholesky.105 = f32[128,128]{1,0:T(8,128)S(1)} custom-call(f32[128,128]{1,0:T(8,128)S(1)} %convolution_subtract_fusion.2), custom_call_target="Cholesky" | custom-call | tf_op jit(solution)/shard_map/jit(cholesky)/cholesky | solution.py:85
  515.1 4.2 while.1
  515.9 1.4 bitcast_dynamic-update-slice_fusion.2
  517.9 1.4 bitcast_dynamic-update-slice_fusion.2
  519.3 19.7 %custom-call.19 = f32[2,128,128]{1,2,0:T(8,128)S(1)} custom-call(f32[2,128,128]{2,1,0:T(8,128)S(1)} %get-tuple-element.10), custom_call_target="InvertDiagBlocksLowerTriangular" | custom-call | tf_op jit(solution)/shard_map/jit(_cho_solve)/triangular_solve | solution.py:86
  540.6 93.1 %reduce-scatter.2.cloned.1.call-done = f32[256,64]{0,1:T(8,128)} async-done(((f32[256,4096]{0,1:T(8,128)}), f32[256,64]{0,1:T(8,128)}) %reduce-scatter.2.cloned.1.call-update) | async-done | bytes 65552 | tf_op jit(solution)/shard_map/reduce_scatter | solution.py:58
  633.7 0.8 convert_element_type.37
  635.4 6.7 %all-to-all-start.2 = ((bf16[8,2,1024]{2,1,0:T(2,128)(2,1)}), bf16[8,2,1024]{2,1,0:T(2,128)(2,1)S(1)}, u32[]{:S(2)}, u32[]{:S(2)}) async-start(bf16[8,2,1024]{2,1,0:T(2,128)(2,1)} %reshape.117), calls=%async_computation.3 | async-start | bytes 65536 | tf_op jit(solution)/shard_map/all_to_all | solution.py:61
  642.8 0.8 copy.53
  643.7 6.5 all-to-all-done.2
  (63 shorter events, 10.8 us)
Async XLA Ops:
  7.2 206.4 %copy-start = (bf16[1,224,4096]{2,1,0:T(8,128)(2,1)S(1)}, bf16[1,224,4096]{2,1,0:T(8,128)(2,1)}, u32[]{:S(2)}) copy-start(bf16[1,224,4096]{2,1,0:T(8,128)(2,1)} %param.12) | copy-start | bytes 5505028
  7.2 107.5 %all-gather.4.cloned.1.call-start = ((), (), s32[]{:S(2)}) async-start(), calls=%async_computation.4 | async-start | bytes 8519680 | tf_op jit(solution)/shard_map/all_gather | solution.py:43
  27.1 177.0 %all-gather.6.cloned.1.call-start = ((), (), s32[]{:S(2)}) async-start(), calls=%async_computation.5 | async-start | bytes 8519680 | tf_op jit(solution)/shard_map/all_gather | solution.py:42
  39.7 248.2 %all-gather.8.cloned.1.call-start = ((), (), s32[]{:S(2)}) async-start(), calls=%async_computation.7 | async-start | bytes 2129920 | tf_op jit(solution)/shard_map/all_gather | solution.py:74
  40.4 437.7 %all-reduce.3.cloned.1.call-start = ((), (), s32[]{:S(2)}) async-start(), calls=%async_computation.8 | async-start | bytes 524288 | tf_op jit(solution)/shard_map/psum | solution.py:83
  213.5 2.6 copy-start.1
  213.5 2.8 copy-start.3
  292.4 341.3 %reduce-scatter.2.cloned.1.call-start = ((), (), s32[]{:S(2)}) async-start(), calls=%async_computation.6 | async-start | bytes 4259840 | tf_op jit(solution)/shard_map/reduce_scatter | solution.py:58
  295.5 0.9 copy-start.2
  635.4 14.8 %all-to-all-start.2 = ((bf16[8,2,1024]{2,1,0:T(2,128)(2,1)}), bf16[8,2,1024]{2,1,0:T(2,128)(2,1)S(1)}, u32[]{:S(2)}, u32[]{:S(2)}) async-start(bf16[8,2,1024]{2,1,0:T(2,128)(2,1)} %reshape.117), calls=%async_computation.3 | async-start | bytes 65536 | tf_op jit(solution)/shard_map/all_to_all | solution.py:61
Sparse Core Ops, SparseCore 0:
  27.3 87.3 all-gather.3
  118.6 85.4 all-gather.5
  207.5 80.3 all-gather.7
  292.5 185.5 all-reduce.2
  482.6 151.0 reduce-scatter.1
where the time goes:
time: 658 us
  waiting for transfers between devices  507 us (77%)
  other arithmetic  58.9 us (9%)
  local copies, waits for them, and re-layouts  28.5 us (4%)
  blocking collectives  25.3 us (4%)
  matrix products  15.3 us (2%)
  between operations  15.3 us (2%)
  starting transfers between devices  7.12 us (1%)
    psum x1, waiting for transfers between devices, per_device(): gram_total = lax.psum(gram_part, 'dp') / total_hidden  181 us
    reduce_scatter x1, waiting for transfers between devices, per_device(): lax.psum_scatter(partial_value, 'dp', scatter_dimension=1, tiled=True)  93.1 us
    all_gather x1, waiting for transfers between devices, per_device(): lax.all_gather(x_recv, 'dp', axis=2, tiled=True)  80.1 us
    all_gather x1, waiting for transfers between devices, per_device(): lax.all_gather(dy_recv, 'dp', axis=2, tiled=True)  74.2 us
    all_gather x1, waiting for transfers between devices, per_device(): basis_full = lax.all_gather(basis, 'dp', axis=0, tiled=True)  70.8 us
    another operation x6, other arithmetic, per_device(): jnp.linalg.cholesky(merged + damping * jnp.eye(merged.shape[0], dtype=jnp...  34 us
    another operation x3, other arithmetic, per_device(): solved = damping * jax.scipy.linalg.cho_solve((factor, True), coefficients)  19.7 us
    all_to_all x1, blocking collectives, per_device(): lax.all_to_all(dy_send, 'expert', split_axis=0, concat_axis=0, tiled=True)  14.9 us
  transfers between devices with their start and end apart: 6, of which 6 were waited for; matrix products, arithmetic and copies ran while one was open for 14% of the time, Pallas kernels for 0%

commit v1 on v0

--- a/solution.py
+++ b/solution.py
@@ -39,7 +39,9 @@
         lax.all_to_all(dy_send, "expert", split_axis=0, concat_axis=0, tiled=True),
     )
     x_full, dy_full = (
-        lax.all_gather(x_recv, "dp", axis=2, tiled=True),
+        jnp.concatenate(
+            lax.all_to_all(jnp.stack([x_recv] * lax.axis_size("dp")), "dp", 0, 0), axis=2
+        ),
         lax.all_gather(dy_recv, "dp", axis=2, tiled=True),
     )
     row_block = x_full.reshape(slot_count, -1)

time: 658 us -> 587 us (0.89)
  waiting for transfers between devices: 507 us -> 399 us
  local copies, waits for them, and re-layouts: 28.5 us -> 50.6 us
  starting transfers between devices: 7.12 us -> 21.4 us
    all_gather x1 -> x0, waiting for transfers between devices: 80.1 us -> none  [per_device(): lax.all_gather(x_recv, 'dp', axis=2, tiled=True)]
    all_gather x1, waiting for transfers between devices: 74.2 us -> 0.01 us  [per_device(): lax.all_gather(dy_recv, 'dp', axis=2, tiled=True)]
    all_to_all x0 -> x1, waiting for transfers between devices: none -> 62.2 us  [per_device(): lax.all_to_all(jnp.stack([x_recv] * lax.axis_size('dp')), 'dp', 0, 0)]
    all_gather x1, waiting for transfers between devices: 70.8 us -> 54.7 us  [per_device(): basis_full = lax.all_gather(basis, 'dp', axis=0, tiled=True)]
    unnamed x16 -> x18, local copies, waits for them, and re-layouts: 3.36 us -> 19.2 us
    all_to_all x0 -> x1, starting transfers between devices: none -> 14.1 us  [per_device(): lax.all_to_all(jnp.stack([x_recv] * lax.axis_size('dp')), 'dp', 0, 0)]
    another operation x6 -> x8, local copies, waits for them, and re-layouts: 3.96 us -> 13.6 us  [the longest x1 6.61 us: per_device(): row_block = x_full.reshape(slot_count, -1)]
    all_gather x1 -> x0, local copies, waits for them, and re-layouts: 9.39 us -> none  [per_device(): lax.all_gather(x_recv, 'dp', axis=2, tiled=True)]
  transfers between devices with their start and end apart: 6 -> 6, of which waited for: 6 -> 5; matrix products, arithmetic and copies ran while one was open for 14% -> 19% of each run, Pallas kernels for 0% -> 0%
where the time goes in v1:
time: 587 us; the launch traced here: 586 us
  waiting for transfers between devices  399 us (68%)
  other arithmetic  58.9 us (10%)
  local copies, waits for them, and re-layouts  50.6 us (9%)
  blocking collectives  25.3 us (4%)
  starting transfers between devices  21.4 us (4%)
  matrix products  15.3 us (3%)
  between operations  15.3 us (3%)
    psum x1, waiting for transfers between devices, per_device(): gram_total = lax.psum(gram_part, 'dp') / total_hidden  181 us
    reduce_scatter x1, waiting for transfers between devices, per_device(): lax.psum_scatter(partial_value, 'dp', scatter_dimension=1, tiled=True)  93.1 us
    all_to_all x1, waiting for transfers between devices, per_device(): lax.all_to_all(jnp.stack([x_recv] * lax.axis_size('dp')), 'dp', 0, 0)  62.2 us
    all_gather x1, waiting for transfers between devices, per_device(): basis_full = lax.all_gather(basis, 'dp', axis=0, tiled=True)  54.7 us
    another operation x6, other arithmetic, per_device(): jnp.linalg.cholesky(merged + damping * jnp.eye(merged.shape[0], dtype=jnp...  34 us
    another operation x3, other arithmetic, per_device(): solved = damping * jax.scipy.linalg.cho_solve((factor, True), coefficients)  19.7 us
    unnamed x18, local copies, waits for them, and re-layouts  19.2 us
    all_to_all x1, blocking collectives, per_device(): lax.all_to_all(dy_send, 'expert', split_axis=0, concat_axis=0, tiled=True)  14.9 us
  transfers between devices with their start and end apart: 6, of which 5 were waited for; matrix products, arithmetic and copies ran while one was open for 19% of the time, Pallas kernels for 0%

profile of v1, /device:TPU:2, one launch (start us, length us, event | category | flops | bytes accessed | tf_op | source)
XLA Modules:
  0.0 585.7 jit_solution(10869261103043856527)
XLA Ops:
  10.1 0.9 fusion.16
  11.3 14.9 %all_to_all.20 = bf16[8,2,1024]{2,1,0:T(2,128)(2,1)S(1)} all-to-all(bf16[8,2,1024]{2,1,0:T(2,128)(2,1)S(1)} %reshape.115), channel_id=1, replica_groups=mesh['dp'=64,'expert'=8] {'expert'}, dimensions={0} | all-to-all | bytes 65536 | tf_op jit(solution)/shard_map/all_to_all | solution.py:39
  27.1 0.9 convolution_convert_fusion.1
  28.3 10.4 %all_to_all.21 = bf16[8,2,1024]{2,1,0:T(2,128)(2,1)S(1)} all-to-all(bf16[8,2,1024]{2,1,0:T(2,128)(2,1)S(1)} %reshape.117), channel_id=1, replica_groups=mesh['dp'=64,'expert'=8] {'expert'}, dimensions={0} | all-to-all | bytes 65536 | tf_op jit(solution)/shard_map/all_to_all | solution.py:38
  38.8 3.0 stack.11
  41.8 7.9 %reshape.119 = bf16[64,2,8192]{2,1,0:T(2,128)(2,1)} reshape(bf16[64,8,32,64]{3,2,1,0:T(8,128)(2,1)} %stack.11) | data formatting | bytes 4194304
  49.7 14.1 %all-to-all-start.2 = ((bf16[64,2,8192]{2,1,0:T(2,128)(2,1)}), bf16[64,2,8192]{2,1,0:T(2,128)(2,1)}, u32[]{:S(2)}, u32[]{:S(2)}) async-start(bf16[64,2,8192]{2,1,0:T(2,128)(2,1)} %reshape.119), calls=%async_computation.2 | async-start | bytes 4194304 | tf_op jit(solution)/shard_map/all_to_all | solution.py:43
  64.7 62.2 %all-to-all-done.2 = bf16[64,2,8192]{2,1,0:T(2,128)(2,1)} async-done(((bf16[64,2,8192]{2,1,0:T(2,128)(2,1)}), bf16[64,2,8192]{2,1,0:T(2,128)(2,1)}, u32[]{:S(2)}, u32[]{:S(2)}) %all-to-all-start.2) | async-done | bytes 2097184 | tf_op jit(solution)/shard_map/all_to_all | solution.py:43
  126.9 8.0 %reshape.120 = bf16[64,8,32,64]{3,2,1,0:T(8,128)(2,1)} reshape(bf16[64,2,8192]{2,1,0:T(2,128)(2,1)} %all-to-all-done.2) | data formatting | bytes 4194304
  134.9 6.8 %copy.47 = bf16[8,32,64,64]{3,2,1,0:T(8,128)(2,1)} copy(bf16[8,32,64,64]{3,1,0,2:T(8,128)(2,1)} %bitcast.87) | data formatting | bytes 4194304 | tf_op jit(solution)/shard_map/reshape | solution.py:42
  141.7 6.6 %reshape_reshape.3 = bf16[256,4096]{1,0:T(8,128)(2,1)} reshape(bf16[8,32,64,64]{3,2,1,0:T(8,128)(2,1)} %copy.47) | data formatting | bytes 4194304 | tf_op jit(solution)/shard_map/reshape;reshape | solution.py:47
  148.3 9.3 %copy.45 = bf16[8,32,4096]{2,1,0:T(8,128)(2,1)} copy(bf16[8,32,4096]{1,0,2:T(8,128)(2,1)} %all-gather.3.cloned.1.call-done) | data formatting | bytes 4194304 | tf_op jit(solution)/shard_map/all_gather | solution.py:45
  157.7 2.5 fusion.2
  161.3 54.7 %all-gather.5.cloned.1.call-done = bf16[4096,256]{1,0:T(8,128)(2,1)} async-done(((bf16[64,256]{1,0:T(8,128)(2,1)}), bf16[4096,256]{1,0:T(8,128)(2,1)}) %all-gather.5.cloned.1.call-update) | async-done | bytes 2097168 | tf_op jit(solution)/shard_map/all_gather | solution.py:76
  216.0 3.1 fusion.15
  219.1 1.3 fusion.34
  220.7 2.9 fusion
  223.7 0.9 copy-done.2
  224.7 181.4 %all-reduce.3.cloned.1.call-done = f32[256,256]{0,1:T(8,128)} async-done(((f32[256,256]{0,1:T(8,128)}), f32[256,256]{0,1:T(8,128)}) %all-reduce.3.cloned.1.call-update) | async-done | bytes 262160 | tf_op jit(solution)/shard_map/psum | solution.py:85
  406.2 1.0 convert_add_fusion
  407.4 11.7 %cholesky.50 = f32[128,128]{1,0:T(8,128)S(1)} custom-call(f32[128,128]{1,0:T(8,128)S(1)} %cholesky.118), custom_call_target="Cholesky" | custom-call | tf_op jit(solution)/shard_map/jit(cholesky)/cholesky | solution.py:87
  419.1 9.8 %custom-call.18 = f32[1,128,128]{1,2,0:T(8,128)S(1)} custom-call(f32[1,128,128]{2,1,0:T(8,128)S(1)} %get-tuple-element.42), custom_call_target="InvertDiagBlocksLowerTriangular" | custom-call | tf_op jit(solution)/shard_map/jit(cholesky)/cholesky | solution.py:87
  429.5 11.7 %cholesky.105 = f32[128,128]{1,0:T(8,128)S(1)} custom-call(f32[128,128]{1,0:T(8,128)S(1)} %convolution_subtract_fusion.2), custom_call_target="Cholesky" | custom-call | tf_op jit(solution)/shard_map/jit(cholesky)/cholesky | solution.py:87
  443.3 4.2 while.1
  444.1 1.4 bitcast_dynamic-update-slice_fusion.2
  446.1 1.4 bitcast_dynamic-update-slice_fusion.2
  447.5 19.7 %custom-call.19 = f32[2,128,128]{1,2,0:T(8,128)S(1)} custom-call(f32[2,128,128]{2,1,0:T(8,128)S(1)} %get-tuple-element.10), custom_call_target="InvertDiagBlocksLowerTriangular" | custom-call | tf_op jit(solution)/shard_map/jit(_cho_solve)/triangular_solve | solution.py:88
  468.7 93.1 %reduce-scatter.2.cloned.1.call-done = f32[256,64]{0,1:T(8,128)} async-done(((f32[256,4096]{0,1:T(8,128)}), f32[256,64]{0,1:T(8,128)}) %reduce-scatter.2.cloned.1.call-update) | async-done | bytes 65552 | tf_op jit(solution)/shard_map/reduce_scatter | solution.py:60
  561.9 0.8 convert_element_type.37
  563.5 6.7 %all-to-all-start.3 = ((bf16[8,2,1024]{2,1,0:T(2,128)(2,1)}), bf16[8,2,1024]{2,1,0:T(2,128)(2,1)S(1)}, u32[]{:S(2)}, u32[]{:S(2)}) async-start(bf16[8,2,1024]{2,1,0:T(2,128)(2,1)} %reshape.121), calls=%async_computation.4 | async-start | bytes 65536 | tf_op jit(solution)/shard_map/all_to_all | solution.py:63
  571.0 0.8 copy.52
  571.8 6.5 %all-to-all-done.3 = bf16[8,2,1024]{2,1,0:T(2,128)(2,1)S(1)} async-done(((bf16[8,2,1024]{2,1,0:T(2,128)(2,1)}), bf16[8,2,1024]{2,1,0:T(2,128)(2,1)S(1)}, u32[]{:S(2)}, u32[]{:S(2)}) %all-to-all-start.3) | async-done | bytes 32800 | tf_op jit(solution)/shard_map/all_to_all | solution.py:63
  (65 shorter events, 13.4 us)
Async XLA Ops:
  7.2 150.5 %copy-start = (bf16[1,224,4096]{2,1,0:T(8,128)(2,1)S(1)}, bf16[1,224,4096]{2,1,0:T(8,128)(2,1)}, u32[]{:S(2)}) copy-start(bf16[1,224,4096]{2,1,0:T(8,128)(2,1)} %param.12) | copy-start | bytes 5505028
  7.2 141.2 %all-gather.3.cloned.1.call-start = ((), (), s32[]{:S(2)}) async-start(), calls=%async_computation.5 | async-start | bytes 8519680 | tf_op jit(solution)/shard_map/all_gather | solution.py:45
  49.7 77.2 %all-to-all-start.2 = ((bf16[64,2,8192]{2,1,0:T(2,128)(2,1)}), bf16[64,2,8192]{2,1,0:T(2,128)(2,1)}, u32[]{:S(2)}, u32[]{:S(2)}) async-start(bf16[64,2,8192]{2,1,0:T(2,128)(2,1)} %reshape.119), calls=%async_computation.2 | async-start | bytes 4194304 | tf_op jit(solution)/shard_map/all_to_all | solution.py:43
  63.7 152.2 %all-gather.5.cloned.1.call-start = ((), (), s32[]{:S(2)}) async-start(), calls=%async_computation.7 | async-start | bytes 2129920 | tf_op jit(solution)/shard_map/all_gather | solution.py:76
  64.5 341.7 %all-reduce.3.cloned.1.call-start = ((), (), s32[]{:S(2)}) async-start(), calls=%async_computation.8 | async-start | bytes 524288 | tf_op jit(solution)/shard_map/psum | solution.py:85
  157.7 2.5 copy-start.1
  157.7 2.8 copy-start.3
  220.5 341.4 %reduce-scatter.2.cloned.1.call-start = ((), (), s32[]{:S(2)}) async-start(), calls=%async_computation.6 | async-start | bytes 4259840 | tf_op jit(solution)/shard_map/reduce_scatter | solution.py:60
  223.6 0.9 copy-start.2
  563.5 14.8 %all-to-all-start.3 = ((bf16[8,2,1024]{2,1,0:T(2,128)(2,1)}), bf16[8,2,1024]{2,1,0:T(2,128)(2,1)S(1)}, u32[]{:S(2)}, u32[]{:S(2)}) async-start(bf16[8,2,1024]{2,1,0:T(2,128)(2,1)} %reshape.121), calls=%async_computation.4 | async-start | bytes 65536 | tf_op jit(solution)/shard_map/all_to_all | solution.py:63
Sparse Core Ops, SparseCore 0:
  27.3 108.4 all-gather.2
  139.1 76.7 all-gather.4
  220.6 185.5 all-reduce.2
  410.7 151.0 reduce-scatter.1
